TPU v7x, 32 devices: a whole 2x2x4 slice. The times are simulated.
32 devices in a mesh: row: 2 (over core), col: 4 (over z), depth: 4 (over y, x).
Axes of the slice: x: 2, y: 2, z: 4, core: 2. Of those that a mesh axis runs over, the one named last changes fastest.
Arguments:
- tokens: bfloat16 [768, 4096], P(('col', 'depth'), 'row'), may hold values from -6 to 6
- cotangent: bfloat16 [768, 4096], P(('col', 'depth'), 'row'), may hold values from -6 to 6
- gate_weight: bfloat16 [4096, 14336], P(('row', 'depth'), 'col'), may hold values from -0.09375 to 0.09375
- up_weight: bfloat16 [4096, 14336], P(('row', 'depth'), 'col'), may hold values from -0.09375 to 0.09375
- down_weight: bfloat16 [14336, 4096], P('col', ('row', 'depth')), may hold values from -0.046875 to 0.046875
Outputs:
- output: bfloat16 [768, 4096], P(('col', 'depth'), 'row')
- input_grad: bfloat16 [768, 4096], P(('col', 'depth'), 'row')
- gate_grad: float32 [4096, 14336], P(('row', 'depth'), 'col')
- up_grad: float32 [4096, 14336], P(('row', 'depth'), 'col')
- down_grad: float32 [14336, 4096], P('col', ('row', 'depth'))
All inputs are finite; a program needn't handle non-finite values.
Results may differ from a plain program's by a relative error of at most 0.0049.
Values may be sent and summed in bfloat16 or wider, within the bound.
No kernel may reach another device: no remote copies, remote signals or barrier semaphores. Data moves between devices by JAX's collectives and lax.ppermute only.
A program may use at most 192 MiB of HBM per device.

v0:
```python
import jax
import jax.numpy as jnp
from jax import lax
from jax.sharding import PartitionSpec as P


def dot_tn(left, right):
    return lax.dot_general(
        left, right, (((0,), (0,)), ((), ())), preferred_element_type=jnp.float32
    )


def dot_nt(left, right):
    return lax.dot_general(
        left, right, (((1,), (1,)), ((), ())), preferred_element_type=jnp.float32
    )


def deltas(hidden_grad, gate, up):
    sig = jax.nn.sigmoid(gate)
    gate_delta = (hidden_grad * up * sig * (1.0 + gate * (1.0 - sig))).astype(jnp.bfloat16)
    up_delta = (hidden_grad * gate * sig).astype(jnp.bfloat16)
    return (gate_delta, up_delta)


def activate(gate, up):
    return (gate * jax.nn.sigmoid(gate) * up).astype(jnp.bfloat16)


def on_device(tokens, cotangent, gate_weight, up_weight, down_weight):
    gate_full, up_full = (
        lax.all_gather(gate_weight, "depth", axis=0, tiled=True),
        lax.all_gather(up_weight, "depth", axis=0, tiled=True),
    )
    down_full = lax.all_gather(down_weight, "depth", axis=1, tiled=True)
    tok_rows, cot_rows = (
        lax.all_gather(tokens, "col", axis=0, tiled=True),
        lax.all_gather(cotangent, "col", axis=0, tiled=True),
    )
    gate = lax.psum_scatter(
        jnp.dot(tok_rows, gate_full, preferred_element_type=jnp.float32),
        "row",
        scatter_dimension=0,
        tiled=True,
    )
    up = lax.psum_scatter(
        jnp.dot(tok_rows, up_full, preferred_element_type=jnp.float32),
        "row",
        scatter_dimension=0,
        tiled=True,
    )
    hid_rows = lax.all_gather(activate(gate, up), "row", axis=0, tiled=True)
    hidden_grad = lax.psum_scatter(
        dot_nt(cot_rows, down_full), "row", scatter_dimension=0, tiled=True
    )
    gate_delta, up_delta = deltas(hidden_grad, gate, up)
    gd_rows, ud_rows = (
        lax.all_gather(gate_delta, "row", axis=0, tiled=True),
        lax.all_gather(up_delta, "row", axis=0, tiled=True),
    )
    output = lax.psum_scatter(
        jnp.dot(hid_rows, down_full, preferred_element_type=jnp.float32),
        "col",
        scatter_dimension=0,
        tiled=True,
    ).astype(jnp.bfloat16)
    input_grad = lax.psum_scatter(
        dot_nt(gd_rows, gate_full) + dot_nt(ud_rows, up_full),
        "col",
        scatter_dimension=0,
        tiled=True,
    ).astype(jnp.bfloat16)
    tok_part, cot_part = (
        lax.all_to_all(tok_rows, "depth", split_axis=1, concat_axis=0, tiled=True),
        lax.all_to_all(cot_rows, "depth", split_axis=1, concat_axis=0, tiled=True),
    )
    gd_all, ud_all, hid_all = (
        lax.all_gather(gd_rows, "depth", axis=0, tiled=True),
        lax.all_gather(ud_rows, "depth", axis=0, tiled=True),
        lax.all_gather(hid_rows, "depth", axis=0, tiled=True),
    )
    gate_grad = dot_tn(tok_part, gd_all)
    up_grad = dot_tn(tok_part, ud_all)
    down_grad = dot_tn(hid_all, cot_part)
    return (output, input_grad, gate_grad, up_grad, down_grad)


def solution(mesh):
    return jax.shard_map(
        on_device,
        mesh=mesh,
        in_specs=(
            P(("col", "depth"), "row"),
            P(("col", "depth"), "row"),
            P(("row", "depth"), "col"),
            P(("row", "depth"), "col"),
            P("col", ("row", "depth")),
        ),
        out_specs=(
            P(("col", "depth"), "row"),
            P(("col", "depth"), "row"),
            P(("row", "depth"), "col"),
            P(("row", "depth"), "col"),
            P("col", ("row", "depth")),
        ),
        check_vma=False,
    )
```

profile of v0, /device:TPU:0, one launch (start us, length us, event | category | flops | bytes accessed | tf_op | source)
XLA Modules:
  0.0 807.5 jit_solution(1116714497966719239)
XLA Ops:
  9.6 21.3 %all_gather.33 = bf16[192,2048]{1,0:T(8,128)(2,1)S(1)} all-gather(bf16[48,2048]{1,0:T(8,128)(2,1)S(1)} %copy-done), channel_id=1, replica_groups=mesh['row'=2,'col'=4,'depth'=4] {'col'}, dimensions={0}, use_global_device_ids=true | all-gather | bytes 983040 | tf_op jit(solution)/shard_map/all_gather | solution.py:37
  30.9 121.7 %all-gather.10.cloned.1.call-done = bf16[2048,3584]{1,0:T(8,128)(2,1)} async-done(((bf16[512,3584]{1,0:T(8,128)(2,1)}), bf16[2048,3584]{1,0:T(8,128)(2,1)}) %all-gather.10.cloned.1.call-update) | async-done | bytes 14680080 | tf_op jit(solution)/shard_map/all_gather | solution.py:32
  152.5 9.8 %fusion = f32[192,3584]{1,0:T(8,128)} fusion(bf16[192,2048]{1,0:T(8,128)(2,1)S(1)} %all_gather.33, bf16[2048,3584]{1,0:T(8,128)(2,1)} %all-gather.10.cloned.1.call-done), kind=kOutput, calls=%fused_computation.9 | convolution fusion | flops 2818572288 | bytes 18219008 | tf_op jit(solution)/shard_map/dot_general | solution.py:41
  162.4 132.0 %all-gather.12.cloned.1.call-done = bf16[2048,3584]{1,0:T(8,128)(2,1)} async-done(((bf16[512,3584]{1,0:T(8,128)(2,1)}), bf16[2048,3584]{1,0:T(8,128)(2,1)}) %all-gather.12.cloned.1.call-update) | async-done | bytes 14680080 | tf_op jit(solution)/shard_map/all_gather | solution.py:33
  294.4 9.8 %fusion.1 = f32[192,3584]{1,0:T(8,128)} fusion(bf16[192,2048]{1,0:T(8,128)(2,1)S(1)} %all_gather.33, bf16[2048,3584]{1,0:T(8,128)(2,1)} %all-gather.12.cloned.1.call-done), kind=kOutput, calls=%fused_computation.10 | convolution fusion | flops 2818572288 | bytes 18219008 | tf_op jit(solution)/shard_map/dot_general | solution.py:47
  305.2 19.5 %all_gather.38 = bf16[192,2048]{1,0:T(8,128)(2,1)S(1)} all-gather(bf16[48,2048]{1,0:T(8,128)(2,1)S(1)} %copy-done.1), channel_id=1, replica_groups=mesh['row'=2,'col'=4,'depth'=4] {'col'}, dimensions={0}, use_global_device_ids=true | all-gather | bytes 983040 | tf_op jit(solution)/shard_map/all_gather | solution.py:38
  324.7 111.3 %all-gather.16.cloned.1.call-done = bf16[3584,2048]{1,0:T(8,128)(2,1)} async-done(((bf16[3584,512]{1,0:T(8,128)(2,1)}), bf16[3584,2048]{1,0:T(8,128)(2,1)}) %all-gather.16.cloned.1.call-update) | async-done | bytes 14680080 | tf_op jit(solution)/shard_map/all_gather | solution.py:35
  436.1 11.7 %fusion.3 = f32[192,3584]{1,0:T(8,128)} fusion(bf16[192,2048]{1,0:T(8,128)(2,1)S(1)} %all_gather.38, bf16[3584,2048]{1,0:T(8,128)(2,1)} %all-gather.16.cloned.1.call-done), kind=kOutput, calls=%fused_computation.12 | convolution fusion | flops 2818572288 | bytes 18219008 | tf_op jit(solution)/shard_map/dot_general | solution.py:14
  447.8 1.3 reduce-scatter.6.cloned.1.call-done
  449.1 14.3 %reduce-scatter.8.cloned.1.call-done = f32[96,3584]{1,0:T(8,128)} async-done(((f32[192,3584]{1,0:T(8,128)}), f32[96,3584]{1,0:T(8,128)}) %reduce-scatter.8.cloned.1.call-update) | async-done | bytes 1376272 | tf_op jit(solution)/shard_map/reduce_scatter | solution.py:46
  463.5 14.3 %reduce-scatter.12.cloned.1.call-done = f32[96,3584]{1,0:T(8,128)} async-done(((f32[192,3584]{1,0:T(8,128)}), f32[96,3584]{1,0:T(8,128)}) %reduce-scatter.12.cloned.1.call-update) | async-done | bytes 1376272 | tf_op jit(solution)/shard_map/reduce_scatter | solution.py:53
  477.8 4.2 multiply_convert_fusion
  483.7 9.2 %all-gather.18.cloned.1.call-done = bf16[192,3584]{1,0:T(8,128)(2,1)} async-done(((bf16[96,3584]{1,0:T(8,128)(2,1)}), bf16[192,3584]{1,0:T(8,128)(2,1)}) %all-gather.18.cloned.1.call-update) | async-done | bytes 1376272 | tf_op jit(solution)/shard_map/all_gather | solution.py:58
  492.9 8.5 %fusion.4 = f32[192,2048]{1,0:T(8,128)S(1)} fusion(bf16[192,3584]{1,0:T(8,128)(2,1)} %all-gather.18.cloned.1.call-done, bf16[2048,3584]{1,0:T(8,128)(2,1)} %all-gather.10.cloned.1.call-done), kind=kOutput, calls=%fused_computation.13 | convolution fusion | flops 2818572288 | bytes 17629184 | tf_op jit(solution)/shard_map/dot_general | solution.py:14
  501.4 4.5 all-gather.20.cloned.1.call-done
  505.9 11.6 %convolution_add_fusion = f32[192,2048]{1,0:T(8,128)} fusion(f32[192,2048]{1,0:T(8,128)S(1)} %fusion.4, bf16[192,3584]{1,0:T(8,128)(2,1)} %all-gather.20.cloned.1.call-done, bf16[2048,3584]{1,0:T(8,128)(2,1)} %all-gather.12.cloned.1.call-done), kind=kOutput, calls=%fused_computation.2 | convolution fusion | flops 2818965504 | bytes 19202048 | tf_op jit(solution)/shard_map/dot_general | solution.py:14
  517.6 1.2 all-gather.14.cloned.1.call-done
  518.8 9.8 %fusion.2 = f32[192,2048]{1,0:T(8,128)} fusion(bf16[192,3584]{1,0:T(8,128)(2,1)} %all-gather.14.cloned.1.call-done, bf16[3584,2048]{1,0:T(8,128)(2,1)} %all-gather.16.cloned.1.call-done), kind=kOutput, calls=%fused_computation.11 | convolution fusion | flops 2818572288 | bytes 17629184 | tf_op jit(solution)/shard_map/dot_general | solution.py:62
  531.5 3.9 all-to-all-start
  536.3 21.8 %reduce-scatter.14.cloned.1.call-done = f32[48,2048]{1,0:T(8,128)} async-done(((f32[192,2048]{1,0:T(8,128)}), f32[48,2048]{1,0:T(8,128)}) %reduce-scatter.14.cloned.1.call-update) | async-done | bytes 393232 | tf_op jit(solution)/shard_map/reduce_scatter | solution.py:67
  558.1 1.7 convert_element_type.19
  559.8 35.6 %reduce-scatter.10.cloned.1.call-done = f32[48,2048]{1,0:T(8,128)} async-done(((f32[192,2048]{1,0:T(8,128)}), f32[48,2048]{1,0:T(8,128)}) %reduce-scatter.10.cloned.1.call-update) | async-done | bytes 393232 | tf_op jit(solution)/shard_map/reduce_scatter | solution.py:61
  595.4 1.7 convert_element_type.16
  597.1 3.7 all-to-all-start.1
  600.8 61.3 %all-gather.22.cloned.1.call-done = bf16[768,3584]{1,0:T(8,128)(2,1)} async-done(((bf16[192,3584]{1,0:T(8,128)(2,1)}), bf16[768,3584]{1,0:T(8,128)(2,1)}) %all-gather.22.cloned.1.call-update) | async-done | bytes 5505040 | tf_op jit(solution)/shard_map/all_gather | solution.py:78
  662.1 7.7 convolution_bitcast_fusion.1
  669.8 8.8 %copy.20 = f32[512,3584]{1,0:T(8,128)} copy(f32[512,3584]{0,1:T(8,128)} %convolution_bitcast_fusion.1) | data formatting | bytes 14680064
  678.6 49.2 %all-gather.24.cloned.1.call-done = bf16[768,3584]{1,0:T(8,128)(2,1)} async-done(((bf16[192,3584]{1,0:T(8,128)(2,1)}), bf16[768,3584]{1,0:T(8,128)(2,1)}) %all-gather.24.cloned.1.call-update) | async-done | bytes 5505040 | tf_op jit(solution)/shard_map/all_gather | solution.py:79
  727.8 7.7 convolution_bitcast_fusion
  735.4 8.7 %copy.21 = f32[512,3584]{1,0:T(8,128)} copy(f32[512,3584]{0,1:T(8,128)} %convolution_bitcast_fusion) | data formatting | bytes 14680064
  744.2 49.1 %all-gather.26.cloned.1.call-done = bf16[768,3584]{1,0:T(8,128)(2,1)} async-done(((bf16[192,3584]{1,0:T(8,128)(2,1)}), bf16[768,3584]{1,0:T(8,128)(2,1)}) %all-gather.26.cloned.1.call-update) | async-done | bytes 5505040 | tf_op jit(solution)/shard_map/all_gather | solution.py:80
  793.2 7.7 fusion.5
  (36 shorter events, 9.0 us)
Async XLA Ops:
  7.2 145.4 %all-gather.10.cloned.1.call-start = ((), (), s32[]{:S(2)}) async-start(), calls=%async_computation.7 | async-start | bytes 18350080 | tf_op jit(solution)/shard_map/all_gather | solution.py:32
  7.9 286.5 %all-gather.12.cloned.1.call-start = ((), (), s32[]{:S(2)}) async-start(), calls=%async_computation.9 | async-start | bytes 18350080 | tf_op jit(solution)/shard_map/all_gather | solution.py:33
  8.6 0.9 copy-start
  8.7 427.4 %all-gather.16.cloned.1.call-start = ((), (), s32[]{:S(2)}) async-start(), calls=%async_computation.12 | async-start | bytes 18350080 | tf_op jit(solution)/shard_map/all_gather | solution.py:35
  9.4 439.7 %reduce-scatter.6.cloned.1.call-start = ((), (), s32[]{:S(2)}) async-start(), calls=%async_computation.8 | async-start | bytes 4128768 | tf_op jit(solution)/shard_map/reduce_scatter | solution.py:40
  162.4 301.1 %reduce-scatter.8.cloned.1.call-start = ((), (), s32[]{:S(2)}) async-start(), calls=%async_computation.10 | async-start | bytes 4128768 | tf_op jit(solution)/shard_map/reduce_scatter | solution.py:46
  304.2 1.0 copy-start.1
  304.2 173.5 %reduce-scatter.12.cloned.1.call-start = ((), (), s32[]{:S(2)}) async-start(), calls=%async_computation.14 | async-start | bytes 4128768 | tf_op jit(solution)/shard_map/reduce_scatter | solution.py:53
  447.8 45.2 %all-gather.18.cloned.1.call-start = ((), (), s32[]{:S(2)}) async-start(), calls=%async_computation.15 | async-start | bytes 2064384 | tf_op jit(solution)/shard_map/all_gather | solution.py:58
  482.0 23.9 %all-gather.20.cloned.1.call-start = ((), (), s32[]{:S(2)}) async-start(), calls=%async_computation.16 | async-start | bytes 2064384 | tf_op jit(solution)/shard_map/all_gather | solution.py:59
  482.8 36.1 %all-gather.14.cloned.1.call-start = ((), (), s32[]{:S(2)}) async-start(), calls=%async_computation.11 | async-start | bytes 2064384 | tf_op jit(solution)/shard_map/all_gather | solution.py:52
  483.5 74.6 %reduce-scatter.14.cloned.1.call-start = ((), (), s32[]{:S(2)}) async-start(), calls=%async_computation.17 | async-start | bytes 1966080 | tf_op jit(solution)/shard_map/reduce_scatter | solution.py:67
  517.6 77.9 %reduce-scatter.10.cloned.1.call-start = ((), (), s32[]{:S(2)}) async-start(), calls=%async_computation.13 | async-start | bytes 1966080 | tf_op jit(solution)/shard_map/reduce_scatter | solution.py:61
  528.6 133.5 %all-gather.22.cloned.1.call-start = ((), (), s32[]{:S(2)}) async-start(), calls=%async_computation.18 | async-start | bytes 6881280 | tf_op jit(solution)/shard_map/all_gather | solution.py:78
  529.2 198.6 %all-gather.24.cloned.1.call-start = ((), (), s32[]{:S(2)}) async-start(), calls=%async_computation.19 | async-start | bytes 6881280 | tf_op jit(solution)/shard_map/all_gather | solution.py:79
  529.9 263.3 %all-gather.26.cloned.1.call-start = ((), (), s32[]{:S(2)}) async-start(), calls=%async_computation.20 | async-start | bytes 6881280 | tf_op jit(solution)/shard_map/all_gather | solution.py:80
  531.5 65.6 %all-to-all-start = ((bf16[192,4,512]{2,0,1:T(8,128)(2,1)}), bf16[192,4,512]{2,0,1:T(8,128)(2,1)S(1)}, u32[]{:S(2)}, u32[]{:S(2)}) async-start(bf16[192,4,512]{2,0,1:T(8,128)(2,1)} %bitcast.35), calls=%async_computation.5 | async-start | bytes 1572864 | tf_op jit(solution)/shard_map/all_to_all | solution.py:74
  597.1 147.1 %all-to-all-start.1 = ((bf16[192,4,512]{2,0,1:T(8,128)(2,1)}), bf16[192,4,512]{2,0,1:T(8,128)(2,1)S(1)}, u32[]{:S(2)}, u32[]{:S(2)}) async-start(bf16[192,4,512]{2,0,1:T(8,128)(2,1)} %bitcast.34), calls=%async_computation.6 | async-start | bytes 1572864 | tf_op jit(solution)/shard_map/all_to_all | solution.py:75
Sparse Core Ops, SparseCore 0:
  9.8 142.6 all-gather.9
  154.4 139.9 all-gather.11
  296.2 139.8 all-gather.15
  438.8 10.3 reduce-scatter.5
  451.9 11.5 reduce-scatter.7
  466.1 11.5 reduce-scatter.11
  482.1 10.7 all-gather.17
  495.1 10.7 all-gather.19
  508.1 10.6 all-gather.13
  521.7 36.4 reduce-scatter.13
  561.1 34.2 reduce-scatter.9
  597.3 64.8 all-gather.21
  664.1 63.6 all-gather.23
  729.6 63.6 all-gather.25
where the time goes:
time: 808 us; the launch traced here: 807 us
  waiting for transfers between devices  632 us (78%)
  matrix products  84.2 us (10%)
  blocking collectives  40.8 us (5%)
  local copies, waits for them, and re-layouts  20.5 us (3%)
  between operations  14 us (2%)
  starting transfers between devices  8.36 us (1%)
    all_gather x1, waiting for transfers between devices, on_device(): lax.all_gather(up_weight, 'depth', axis=0, tiled=True)  132 us
    all_gather x1, waiting for transfers between devices, on_device(): lax.all_gather(gate_weight, 'depth', axis=0, tiled=True)  122 us
    all_gather x1, waiting for transfers between devices, on_device(): down_full = lax.all_gather(down_weight, 'depth', axis=1, tiled=True)  111 us
    all_gather x1, waiting for transfers between devices, on_device(): lax.all_gather(gd_rows, 'depth', axis=0, tiled=True)  61.3 us
    all_gather x1, waiting for transfers between devices, on_device(): lax.all_gather(ud_rows, 'depth', axis=0, tiled=True)  49.2 us
    all_gather x1, waiting for transfers between devices, on_device(): lax.all_gather(hid_rows, 'depth', axis=0, tiled=True)  49.1 us
    reduce_scatter x1, waiting for transfers between devices, on_device(): lax.psum_scatter(jnp.dot(hid_rows, down_full, preferred_element_type=jnp....  35.6 us
    dot_general x3, matrix products, dot_nt(): lax.dot_general(left, right, (((1,), (1,)), ((), ())), preferred_element_...  31.8 us
  transfers between devices with their start and end apart: 16, of which 14 were waited for; matrix products, arithmetic and copies ran while one was open for 12% of the time, Pallas kernels for 0%

commit v1 on v0

--- a/solution.py
+++ b/solution.py
@@ -1,7 +1,27 @@
+import functools
 import jax
 import jax.numpy as jnp
 from jax import lax
 from jax.sharding import PartitionSpec as P
+
+
+def _divide_row(target, across, dim_no):
+    n_dev_all = lax.axis_size(across)
+    stack_in = [target]
+    c = 0
+    while c < n_dev_all - 1:
+        low = lax.ppermute(
+            stack_in[-1], across, [(dev_j, (dev_j + 1) % n_dev_all) for dev_j in range(n_dev_all)]
+        )
+        stack_in.append(low)
+        c = c + 1
+    local_out = jnp.concatenate(stack_in[::-1], axis=dim_no)
+    aux = lax.axis_index(across)
+    extra = jnp.roll(local_out, (aux + 1) * target.shape[dim_no], axis=dim_no)
+    return extra
+
+
+cycles_take = functools.partial(_divide_row, across="depth", dim_no=1)
 
 
 def dot_tn(left, right):
@@ -32,7 +52,7 @@
         lax.all_gather(gate_weight, "depth", axis=0, tiled=True),
         lax.all_gather(up_weight, "depth", axis=0, tiled=True),
     )
-    down_full = lax.all_gather(down_weight, "depth", axis=1, tiled=True)
+    down_full = cycles_take(down_weight)
     tok_rows, cot_rows = (
         lax.all_gather(tokens, "col", axis=0, tiled=True),
         lax.all_gather(cotangent, "col", axis=0, tiled=True),

time: 808 us -> 809 us (level)
  waiting for transfers between devices: 632 us -> 602 us
  local copies, waits for them, and re-layouts: 20.5 us -> 46.3 us
    ppermute x0 -> x3, waiting for transfers between devices: none -> 412 us  [_divide_row(): lax.ppermute(stack_in[-1], across, [(dev_j, (dev_j + 1) % n_dev_all) for...]
    all_gather x1, waiting for transfers between devices: 132 us -> 0.02 us  [on_device(): lax.all_gather(up_weight, 'depth', axis=0, tiled=True)]
    all_gather x1, waiting for transfers between devices: 122 us -> 0.01 us  [on_device(): lax.all_gather(gate_weight, 'depth', axis=0, tiled=True)]
    all_gather x1 -> x0, waiting for transfers between devices: 111 us -> none  [on_device(): down_full = lax.all_gather(down_weight, 'depth', axis=1, tiled=True)]
    all_gather x1, waiting for transfers between devices: 61.3 us -> 0.36 us  [on_device(): lax.all_gather(gd_rows, 'depth', axis=0, tiled=True)]
    unnamed x6 -> x19, local copies, waits for them, and re-layouts: 18.6 us -> 42.3 us
    reduce_scatter x1, waiting for transfers between devices: 35.6 us -> 20 us  [on_device(): lax.psum_scatter(jnp.dot(hid_rows, down_full, preferred_element_type=jnp....]
    reduce_scatter x1, waiting for transfers between devices: 14.3 us -> 0.02 us  [on_device(): lax.psum_scatter(dot_nt(cot_rows, down_full), 'row', scatter_dimension=0,...]
  transfers between devices with their start and end apart: 16 -> 18, of which waited for: 14 -> 13; matrix products, arithmetic and copies ran while one was open for 12% -> 15% of each run, Pallas kernels for 0% -> 0%
where the time goes in v1:
time: 809 us; the launch traced here: 808 us
  waiting for transfers between devices  602 us (74%)
  matrix products  84.1 us (10%)
  local copies, waits for them, and re-layouts  46.3 us (6%)
  blocking collectives  36.3 us (4%)
  starting transfers between devices  16.3 us (2%)
  between operations  15.4 us (2%)
    ppermute x3, waiting for transfers between devices, _divide_row(): lax.ppermute(stack_in[-1], across, [(dev_j, (dev_j + 1) % n_dev_all) for...  412 us
    all_gather x1, waiting for transfers between devices, on_device(): lax.all_gather(ud_rows, 'depth', axis=0, tiled=True)  49.1 us
    all_gather x1, waiting for transfers between devices, on_device(): lax.all_gather(hid_rows, 'depth', axis=0, tiled=True)  49.1 us
    unnamed x19, local copies, waits for them, and re-layouts  42.3 us
    reduce_scatter x1, waiting for transfers between devices, on_device(): lax.psum_scatter(dot_nt(gd_rows, gate_full) + dot_nt(ud_rows, up_full), '...  35.4 us
    dot_general x3, matrix products, dot_nt(): lax.dot_general(left, right, (((1,), (1,)), ((), ())), preferred_element_...  31.9 us
    dot_general x3, matrix products, dot_tn(): lax.dot_general(left, right, (((0,), (0,)), ((), ())), preferred_element_...  23.1 us
    reduce_scatter x1, waiting for transfers between devices, on_device(): lax.psum_scatter(jnp.dot(hid_rows, down_full, preferred_element_type=jnp....  20 us
  transfers between devices with their start and end apart: 18, of which 13 were waited for; matrix products, arithmetic and copies ran while one was open for 15% of the time, Pallas kernels for 0%

profile of v1, /device:TPU:0, one launch (start us, length us, event | category | flops | bytes accessed | tf_op | source)
XLA Modules:
  0.0 808.4 jit_solution(16867777893779885418)
XLA Ops:
  9.5 3.0 collective-permute-start
  12.5 138.5 %collective-permute-done = bf16[3584,512]{1,0:T(8,128)(2,1)S(1)} collective-permute-done((bf16[3584,512]{1,0:T(8,128)(2,1)}, bf16[3584,512]{1,0:T(8,128)(2,1)S(1)}, u32[]{:S(2)}, u32[]{:S(2)}) %collective-permute-start) | collective-permute-done | bytes 3670048 | tf_op jit(solution)/shard_map/ppermute | solution.py:13
  155.2 141.4 %collective-permute-done.1 = bf16[3584,512]{1,0:T(8,128)(2,1)} collective-permute-done((bf16[3584,512]{1,0:T(8,128)(2,1)S(1)}, bf16[3584,512]{1,0:T(8,128)(2,1)}, u32[]{:S(2)}, u32[]{:S(2)}) %collective-permute-start.1) | collective-permute-done | bytes 3670048 | tf_op jit(solution)/shard_map/ppermute | solution.py:13
  299.3 17.8 %all_gather.34 = bf16[192,2048]{1,0:T(8,128)(2,1)S(1)} all-gather(bf16[48,2048]{1,0:T(8,128)(2,1)S(1)} %copy-done.3), channel_id=1, replica_groups=mesh['row'=2,'col'=4,'depth'=4] {'col'}, dimensions={0}, use_global_device_ids=true | all-gather | bytes 983040 | tf_op jit(solution)/shard_map/all_gather | solution.py:58
  317.1 131.7 %collective-permute-done.2 = bf16[3584,512]{1,0:T(8,128)(2,1)} collective-permute-done((bf16[3584,512]{1,0:T(8,128)(2,1)}, bf16[3584,512]{1,0:T(8,128)(2,1)}, u32[]{:S(2)}, u32[]{:S(2)}) %collective-permute-start.2) | collective-permute-done | bytes 3670048 | tf_op jit(solution)/shard_map/ppermute | solution.py:13
  448.8 4.1 constant_dynamic-update-slice_fusion.7
  452.9 4.3 constant_dynamic-update-slice_fusion.6
  461.4 4.1 constant_dynamic-update-slice_fusion.3
  465.5 4.1 constant_dynamic-update-slice_fusion.2
  473.8 11.7 %fusion.4 = f32[192,3584]{1,0:T(8,128)} fusion(bf16[192,2048]{1,0:T(8,128)(2,1)S(1)} %all_gather.34, bf16[3584,4096]{1,0:T(8,128)(2,1)} %constant_dynamic-update-slice_fusion, s32[]{:T(128)S(6)} %select_n.14), kind=kOutput, calls=%fused_computation.6 | convolution fusion | flops 2818572288 | bytes 18219012 | tf_op jit(solution)/shard_map/dot_general | solution.py:34
  485.6 18.5 %all_gather.30 = bf16[192,2048]{1,0:T(8,128)(2,1)S(1)} all-gather(bf16[48,2048]{1,0:T(8,128)(2,1)S(1)} %copy-done.4), channel_id=1, replica_groups=mesh['row'=2,'col'=4,'depth'=4] {'col'}, dimensions={0}, use_global_device_ids=true | all-gather | bytes 983040 | tf_op jit(solution)/shard_map/all_gather | solution.py:57
  504.1 9.7 %fusion.9 = f32[192,3584]{1,0:T(8,128)} fusion(bf16[192,2048]{1,0:T(8,128)(2,1)S(1)} %all_gather.30, bf16[2048,3584]{1,0:T(8,128)(2,1)} %all-gather.9.cloned.1.call-done), kind=kOutput, calls=%fused_computation.24 | convolution fusion | flops 2818572288 | bytes 18219008 | tf_op jit(solution)/shard_map/dot_general | solution.py:61
  513.9 9.7 %fusion.10 = f32[192,3584]{1,0:T(8,128)} fusion(bf16[192,2048]{1,0:T(8,128)(2,1)S(1)} %all_gather.30, bf16[2048,3584]{1,0:T(8,128)(2,1)} %all-gather.11.cloned.1.call-done), kind=kOutput, calls=%fused_computation.25 | convolution fusion | flops 2818572288 | bytes 18219008 | tf_op jit(solution)/shard_map/dot_general | solution.py:67
  525.5 14.2 %reduce-scatter.8.cloned.1.call-done = f32[96,3584]{1,0:T(8,128)} async-done(((f32[192,3584]{1,0:T(8,128)}), f32[96,3584]{1,0:T(8,128)}) %reduce-scatter.8.cloned.1.call-update) | async-done | bytes 1376272 | tf_op jit(solution)/shard_map/reduce_scatter | solution.py:66
  539.8 4.2 multiply_convert_fusion
  545.7 9.0 %all-gather.13.cloned.1.call-done = bf16[192,3584]{1,0:T(8,128)(2,1)} async-done(((bf16[96,3584]{1,0:T(8,128)(2,1)}), bf16[192,3584]{1,0:T(8,128)(2,1)}) %all-gather.13.cloned.1.call-update) | async-done | bytes 1376272 | tf_op jit(solution)/shard_map/all_gather | solution.py:72
  554.8 9.8 %fusion.2 = f32[192,2048]{1,0:T(8,128)} fusion(bf16[192,3584]{1,0:T(8,128)(2,1)} %all-gather.13.cloned.1.call-done, bf16[3584,4096]{1,0:T(8,128)(2,1)} %constant_dynamic-update-slice_fusion, s32[]{:T(128)S(6)} %select_n.14), kind=kOutput, calls=%fused_computation.2 | convolution fusion | flops 2818572288 | bytes 17629188 | tf_op jit(solution)/shard_map/dot_general | solution.py:82
  564.6 3.0 all-gather.15.cloned.1.call-done
  567.6 8.5 %fusion.11 = f32[192,2048]{1,0:T(8,128)S(1)} fusion(bf16[192,3584]{1,0:T(8,128)(2,1)} %all-gather.15.cloned.1.call-done, bf16[2048,3584]{1,0:T(8,128)(2,1)} %all-gather.9.cloned.1.call-done), kind=kOutput, calls=%fused_computation.26 | convolution fusion | flops 2818572288 | bytes 17629184 | tf_op jit(solution)/shard_map/dot_general | solution.py:34
  576.2 4.3 all-gather.17.cloned.1.call-done
  580.5 11.6 %convolution_add_fusion = f32[192,2048]{1,0:T(8,128)} fusion(f32[192,2048]{1,0:T(8,128)S(1)} %fusion.11, bf16[192,3584]{1,0:T(8,128)(2,1)} %all-gather.17.cloned.1.call-done, bf16[2048,3584]{1,0:T(8,128)(2,1)} %all-gather.11.cloned.1.call-done), kind=kOutput, calls=%fused_computation.7 | convolution fusion | flops 2818965504 | bytes 19202048 | tf_op jit(solution)/shard_map/dot_general | solution.py:34
  595.0 3.9 all-to-all-start
  599.9 20.0 %reduce-scatter.10.cloned.1.call-done = f32[48,2048]{1,0:T(8,128)} async-done(((f32[192,2048]{1,0:T(8,128)}), f32[48,2048]{1,0:T(8,128)}) %reduce-scatter.10.cloned.1.call-update) | async-done | bytes 393232 | tf_op jit(solution)/shard_map/reduce_scatter | solution.py:81
  621.5 35.4 %reduce-scatter.14.cloned.1.call-done = f32[48,2048]{1,0:T(8,128)} async-done(((f32[192,2048]{1,0:T(8,128)}), f32[48,2048]{1,0:T(8,128)}) %reduce-scatter.14.cloned.1.call-update) | async-done | bytes 393232 | tf_op jit(solution)/shard_map/reduce_scatter | solution.py:87
  658.6 3.7 all-to-all-start.1
  662.7 7.7 convolution_bitcast_fusion.1
  670.4 8.7 %copy.20 = f32[512,3584]{1,0:T(8,128)} copy(f32[512,3584]{0,1:T(8,128)} %convolution_bitcast_fusion.1) | data formatting | bytes 14680064
  679.1 49.1 %all-gather.21.cloned.1.call-done = bf16[768,3584]{1,0:T(8,128)(2,1)} async-done(((bf16[192,3584]{1,0:T(8,128)(2,1)}), bf16[768,3584]{1,0:T(8,128)(2,1)}) %all-gather.21.cloned.1.call-update) | async-done | bytes 5505040 | tf_op jit(solution)/shard_map/all_gather | solution.py:99
  728.2 7.7 convolution_bitcast_fusion
  735.9 8.7 %copy.21 = f32[512,3584]{1,0:T(8,128)} copy(f32[512,3584]{0,1:T(8,128)} %convolution_bitcast_fusion) | data formatting | bytes 14680064
  744.6 49.1 %all-gather.23.cloned.1.call-done = bf16[768,3584]{1,0:T(8,128)(2,1)} async-done(((bf16[192,3584]{1,0:T(8,128)(2,1)}), bf16[768,3584]{1,0:T(8,128)(2,1)}) %all-gather.23.cloned.1.call-update) | async-done | bytes 5505040 | tf_op jit(solution)/shard_map/all_gather | solution.py:100
  793.6 7.7 fusion.12
  (53 shorter events, 28.0 us)
Async XLA Ops:
  8.0 291.3 %copy-start.3 = (bf16[48,2048]{1,0:T(8,128)(2,1)S(1)}, bf16[48,2048]{1,0:T(8,128)(2,1)}, u32[]{:S(2)}) copy-start(bf16[48,2048]{1,0:T(8,128)(2,1)} %param.6) | copy-start | bytes 589828
  8.0 496.1 %all-gather.9.cloned.1.call-start = ((), (), s32[]{:S(2)}) async-start(), calls=%async_computation.7 | async-start | bytes 18350080 | tf_op jit(solution)/shard_map/all_gather | solution.py:52
  8.7 505.2 %all-gather.11.cloned.1.call-start = ((), (), s32[]{:S(2)}) async-start(), calls=%async_computation.9 | async-start | bytes 18350080 | tf_op jit(solution)/shard_map/all_gather | solution.py:53
  9.5 514.3 %reduce-scatter.12.cloned.1.call-start = ((), (), s32[]{:S(2)}) async-start(), calls=%async_computation.13 | async-start | bytes 4128768 | tf_op jit(solution)/shard_map/reduce_scatter | solution.py:73
  9.5 141.5 %collective-permute-start = (bf16[3584,512]{1,0:T(8,128)(2,1)}, bf16[3584,512]{1,0:T(8,128)(2,1)S(1)}, u32[]{:S(2)}, u32[]{:S(2)}) collective-permute-start(bf16[3584,512]{1,0:T(8,128)(2,1)} %param.9), channel_id=1, source_target_pairs={{0,1},{1,2},{2,3},{3,0},{4,5},{5,6},{6,7},{7,4},{8,9},{9,10},{10,1... | collective-permute-start | bytes 11010056 | tf_op jit(solution)/shard_map/ppermute | solution.py:13
  151.0 1.8 copy-start.1
  152.8 143.8 %collective-permute-start.1 = (bf16[3584,512]{1,0:T(8,128)(2,1)S(1)}, bf16[3584,512]{1,0:T(8,128)(2,1)}, u32[]{:S(2)}, u32[]{:S(2)}) collective-permute-start(bf16[3584,512]{1,0:T(8,128)(2,1)S(1)} %collective-permute-done), channel_id=1, source_target_pairs={{0,1},{1,2},{2,3},{3,0},{4,5},{5,6},{6,7},{7,4},{8,9},{9,10},{10,1... | collective-permute-start | bytes 11010056 | tf_op jit(solution)/shard_map/ppermute | solution.py:13
  296.7 152.1 %collective-permute-start.2 = (bf16[3584,512]{1,0:T(8,128)(2,1)}, bf16[3584,512]{1,0:T(8,128)(2,1)}, u32[]{:S(2)}, u32[]{:S(2)}) collective-permute-start(bf16[3584,512]{1,0:T(8,128)(2,1)} %collective-permute-done.1), channel_id=1, source_target_pairs={{0,1},{1,2},{2,3},{3,0},{4,5},{5,6},{6,7},{7,4},{8,9},{9,10},{10,1... | collective-permute-start | bytes 11010056 | tf_op jit(solution)/shard_map/ppermute | solution.py:13
  452.9 4.3 copy-start.2
  452.9 6.4 copy-start
  473.8 11.8 %copy-start.4 = (bf16[48,2048]{1,0:T(8,128)(2,1)S(1)}, bf16[48,2048]{1,0:T(8,128)(2,1)}, u32[]{:S(2)}) copy-start(bf16[48,2048]{1,0:T(8,128)(2,1)} %param.5) | copy-start | bytes 589828
  485.6 40.0 %reduce-scatter.6.cloned.1.call-start = ((), (), s32[]{:S(2)}) async-start(), calls=%async_computation.8 | async-start | bytes 4128768 | tf_op jit(solution)/shard_map/reduce_scatter | solution.py:60
  513.8 25.9 %reduce-scatter.8.cloned.1.call-start = ((), (), s32[]{:S(2)}) async-start(), calls=%async_computation.10 | async-start | bytes 4128768 | tf_op jit(solution)/shard_map/reduce_scatter | solution.py:66
  523.7 31.1 %all-gather.13.cloned.1.call-start = ((), (), s32[]{:S(2)}) async-start(), calls=%async_computation.11 | async-start | bytes 2064384 | tf_op jit(solution)/shard_map/all_gather | solution.py:72
  544.0 23.6 %all-gather.15.cloned.1.call-start = ((), (), s32[]{:S(2)}) async-start(), calls=%async_computation.14 | async-start | bytes 2064384 | tf_op jit(solution)/shard_map/all_gather | solution.py:78
  544.8 35.7 %all-gather.17.cloned.1.call-start = ((), (), s32[]{:S(2)}) async-start(), calls=%async_computation.15 | async-start | bytes 2064384 | tf_op jit(solution)/shard_map/all_gather | solution.py:79
  545.5 74.3 %reduce-scatter.10.cloned.1.call-start = ((), (), s32[]{:S(2)}) async-start(), calls=%async_computation.12 | async-start | bytes 1966080 | tf_op jit(solution)/shard_map/reduce_scatter | solution.py:81
  564.5 92.4 %reduce-scatter.14.cloned.1.call-start = ((), (), s32[]{:S(2)}) async-start(), calls=%async_computation.16 | async-start | bytes 1966080 | tf_op jit(solution)/shard_map/reduce_scatter | solution.py:87
  592.1 70.5 %all-gather.19.cloned.1.call-start = ((), (), s32[]{:S(2)}) async-start(), calls=%async_computation.17 | async-start | bytes 6881280 | tf_op jit(solution)/shard_map/all_gather | solution.py:98
  592.9 135.3 %all-gather.21.cloned.1.call-start = ((), (), s32[]{:S(2)}) async-start(), calls=%async_computation.18 | async-start | bytes 6881280 | tf_op jit(solution)/shard_map/all_gather | solution.py:99
  593.4 200.2 %all-gather.23.cloned.1.call-start = ((), (), s32[]{:S(2)}) async-start(), calls=%async_computation.19 | async-start | bytes 6881280 | tf_op jit(solution)/shard_map/all_gather | solution.py:100
  595.0 63.6 %all-to-all-start = ((bf16[192,4,512]{2,0,1:T(8,128)(2,1)}), bf16[192,4,512]{2,0,1:T(8,128)(2,1)S(1)}, u32[]{:S(2)}, u32[]{:S(2)}) async-start(bf16[192,4,512]{2,0,1:T(8,128)(2,1)} %bitcast.35), calls=%async_computation.5 | async-start | bytes 1572864 | tf_op jit(solution)/shard_map/all_to_all | solution.py:94
  658.6 86.0 %all-to-all-start.1 = ((bf16[192,4,512]{2,0,1:T(8,128)(2,1)}), bf16[192,4,512]{2,0,1:T(8,128)(2,1)S(1)}, u32[]{:S(2)}, u32[]{:S(2)}) async-start(bf16[192,4,512]{2,0,1:T(8,128)(2,1)} %bitcast.34), calls=%async_computation.6 | async-start | bytes 1572864 | tf_op jit(solution)/shard_map/all_to_all | solution.py:95
Sparse Core Ops, SparseCore 0:
  10.8 256.4 all-gather.8
  269.1 217.6 all-gather.10
  595.0 67.6 all-gather.18
  664.5 63.6 all-gather.20
  730.0 63.6 all-gather.22
Sparse Core Ops, SparseCore 1:
  485.7 12.2 reduce-scatter.11
  513.9 11.5 reduce-scatter.5
  528.2 11.5 reduce-scatter.7
  544.1 10.6 all-gather.12
  557.0 10.6 all-gather.14
  569.8 10.6 all-gather.16
  583.3 36.5 reduce-scatter.9
  622.7 34.1 reduce-scatter.13
